TPU v7x, 32 devices: a whole 2x2x4 slice. The times are simulated.
32 devices in a mesh: dp: 8 (over z, x), tm: 4 (over y, core).
Axes of the slice: x: 2, y: 2, z: 4, core: 2. Of those that a mesh axis runs over, the one named last changes fastest.
Arguments:
- clips: bfloat16 [8, 32, 16, 16, 256], P('dp', 'tm'), may hold values from -6 to 6
- frame_counts: int32 [8], P('dp'), may hold values from 5 to 32, as said below
- weight: bfloat16 [6912, 256], P('dp'), may hold values from -0.078125 to 0.078125
- gain: float32 [256], replicated, may hold values from 0.1 to 1.9
- bias: float32 [256], replicated, may hold values from -3 to 3
- cotangent: bfloat16 [8, 16, 8, 8, 256], P('dp', 'tm'), may hold values from -6 to 6
Outputs:
- output: bfloat16 [8, 16, 8, 8, 256], P('dp', 'tm')
- input_grad: bfloat16 [8, 32, 16, 16, 256], P('dp', 'tm')
- weight_grad: float32 [6912, 256], P('dp')
Inputs may be any that keep to these rules, and one draw needn't show every extreme that they name: frame_counts[c] frames of clip c are valid, the remaining slots are padding; in every draw some clip uses all 32 slots.
All inputs are finite; a program needn't handle non-finite values.
Results may differ from a plain program's by a relative error of at most 0.0048.
Values may be sent and summed in bfloat16 or wider, within the bound.
A program may use at most 64 MiB of HBM per device.

v0:
```python
import jax
import jax.numpy as jnp
from jax import lax
from jax.sharding import PartitionSpec as P

GROUPS = 32
EPS = 1e-06


def shifted(value, axis, by):
    devices = lax.axis_size(axis)
    pairs = [(i, i + by) for i in range(devices) if 0 <= i + by < devices]
    return lax.ppermute(value, axis, pairs)


def unfold(padded, frames_out, rows_out, cols_out):
    tap_list = []
    for step_t in range(3):
        for step_r in range(3):
            for step_c in range(3):
                tap_piece = padded[
                    step_t : step_t + 2 * frames_out : 2,
                    step_r : step_r + 2 * rows_out : 2,
                    step_c : step_c + 2 * cols_out : 2,
                    :,
                ]
                tap_list.append(tap_piece.reshape(frames_out * rows_out * cols_out, -1))
    return jnp.concatenate(tap_list, axis=1)


def spread_taps(values, data_axis, tap_axis, length):
    moved = jnp.moveaxis(values, tap_axis, 0)
    count = moved.shape[data_axis + 1]
    width_list = [(0, 0)] * (moved.ndim - 1)
    after = list(width_list)
    after[data_axis] = (0, 1)
    before = list(width_list)
    before[data_axis] = (1, 0)
    even_part = jnp.pad(moved[0], after) + jnp.pad(moved[2], before)
    odd_part = jnp.pad(moved[1], after)
    joined = jnp.stack([even_part, odd_part], axis=data_axis + 1)
    shape_new = list(even_part.shape)
    shape_new[data_axis] = 2 * (count + 1)
    joined = joined.reshape(shape_new)
    return lax.slice_in_dim(joined, 0, length, axis=data_axis)


def fold_back(columns, padded_shape, frames_out, rows_out, cols_out):
    channels = padded_shape[3]
    blocks = columns.reshape(frames_out, rows_out, cols_out, 3, 3, 3, channels)
    blocks = spread_taps(blocks, 0, 3, padded_shape[0])
    blocks = spread_taps(blocks, 1, 3, padded_shape[1])
    blocks = spread_taps(blocks, 2, 3, padded_shape[2])
    return blocks


def silu_slope(preact):
    sig = jax.nn.sigmoid(preact)
    return sig * (1.0 + preact * (1.0 - sig))


def shards(clips, frame_counts, weight, gain, bias, cotangent):
    clip_data = clips[0]
    cot_block = cotangent[0]
    frame_count, row_count, col_count, channels = clip_data.shape
    width_g = channels // GROUPS
    first_frame = lax.axis_index("tm") * frame_count
    frame_mask = (first_frame + jnp.arange(frame_count) < frame_counts[0]).astype(jnp.float32)[
        :, None, None, None
    ]
    mask_group = frame_mask[..., None]
    entries = frame_counts[0].astype(jnp.float32) * (row_count * col_count * width_g)
    values = clip_data.astype(jnp.float32).reshape(
        frame_count, row_count, col_count, GROUPS, width_g
    )
    sum_first, sum_second = lax.psum(
        (
            jnp.sum(values * mask_group, axis=(0, 1, 2, 4)),
            jnp.sum(values * values * mask_group, axis=(0, 1, 2, 4)),
        ),
        "tm",
    )
    group_mean = sum_first / entries
    variance = sum_second / entries - group_mean * group_mean
    inv_std = lax.rsqrt(variance + EPS)
    normed_g = (values - group_mean[:, None]) * inv_std[:, None]
    normed = normed_g.reshape(frame_count, row_count, col_count, channels)
    preact = normed * gain + bias
    hidden = (jax.nn.silu(preact) * frame_mask).astype(jnp.bfloat16)
    earlier = shifted(hidden[-2:], "tm", 1)
    padded = jnp.pad(jnp.concatenate([earlier, hidden], axis=0), ((0, 0), (1, 0), (1, 0), (0, 0)))
    frames_out, rows_out, cols_out = (frame_count // 2, row_count // 2, col_count // 2)
    patches = unfold(padded, frames_out, rows_out, cols_out)
    cot_rows = cot_block.reshape(-1, channels)
    full_weight = lax.all_gather(weight, "dp", axis=0, tiled=True)
    out_rows = jnp.dot(patches, full_weight, preferred_element_type=jnp.float32)
    out_block = out_rows.astype(jnp.bfloat16).reshape(frames_out, rows_out, cols_out, channels)
    dcols = lax.dot_general(
        cot_rows, full_weight, (((1,), (1,)), ((), ())), preferred_element_type=jnp.float32
    )
    dpad = fold_back(dcols, padded.shape, frames_out, rows_out, cols_out)
    passed = shifted(dpad[:2, 1:, 1:, :], "tm", -1)
    dlocal = dpad[2:, 1:, 1:, :]
    dhidden = jnp.concatenate([dlocal[:-2], dlocal[-2:] + passed], axis=0)
    dnormed = dhidden * frame_mask * silu_slope(preact) * gain
    grad_norm = dnormed.reshape(frame_count, row_count, col_count, GROUPS, width_g)
    back_first, back_second = lax.psum(
        (jnp.sum(grad_norm, axis=(0, 1, 2, 4)), jnp.sum(grad_norm * normed_g, axis=(0, 1, 2, 4))),
        "tm",
    )
    input_grad = (
        mask_group
        * inv_std[:, None]
        * (grad_norm - back_first[:, None] / entries - normed_g * back_second[:, None] / entries)
    )
    input_grad = input_grad.reshape(frame_count, row_count, col_count, channels).astype(
        jnp.bfloat16
    )
    local_grad = lax.dot_general(
        patches, cot_rows, (((0,), (0,)), ((), ())), preferred_element_type=jnp.float32
    )
    clip_grad = lax.psum(local_grad, "tm")
    weight_grad = lax.psum_scatter(clip_grad, "dp", scatter_dimension=0, tiled=True)
    return (out_block[None], input_grad[None], weight_grad)


def solution(mesh):
    placed = (
        P("dp", "tm", None, None, None),
        P("dp"),
        P("dp", None),
        P(),
        P(),
        P("dp", "tm", None, None, None),
    )
    return jax.shard_map(
        shards,
        mesh=mesh,
        in_specs=placed,
        out_specs=(P("dp", "tm", None, None, None), P("dp", "tm", None, None, None), P("dp", None)),
        check_vma=False,
    )
```

profile of v0, /device:TPU:0, one launch (start us, length us, event | category | flops | bytes accessed | tf_op | source)
XLA Modules:
  0.0 398.6 jit_solution(1808083092063788715)
XLA Ops:
  8.6 1.8 fusion.18
  10.9 8.4 %all-reduce.11 = (f32[32]{0:T(128)S(1)}, f32[32]{0:T(128)S(1)}) all-reduce(f32[32]{0:T(128)S(1)} %reduce_sum.51, f32[32]{0:T(128)S(1)} %reduce_sum.54), channel_id=1, replica_groups=mesh['dp'=8,'tm'=4] {'tm'}, use_global_device_ids=true, to_apply=%region_2.0 | all-reduce | flops 64 | bytes 512 | tf_op jit(solution)/shard_map/psum | solution.py:76
  19.6 2.1 fusion.15
  34.1 9.8 %slice.146 = bf16[4,8,8,256]{3,2,1,0:T(8,128)(2,1)} slice(bf16[10,17,17,256]{3,2,1,0:T(8,128)(2,1)S(1)} %fusion.38), slice={[1:9:2], [2:17:2], [1:17:2], [0:256:1]} | slice | bytes 262144 | tf_op jit(solution)/shard_map/slice | solution.py:21
  43.9 9.7 %slice.145 = bf16[4,8,8,256]{3,2,1,0:T(8,128)(2,1)} slice(bf16[10,17,17,256]{3,2,1,0:T(8,128)(2,1)S(1)} %fusion.38), slice={[1:9:2], [2:17:2], [0:16:2], [0:256:1]} | slice | bytes 262144 | tf_op jit(solution)/shard_map/slice | solution.py:21
  53.6 9.8 %slice.144 = bf16[4,8,8,256]{3,2,1,0:T(8,128)(2,1)} slice(bf16[10,17,17,256]{3,2,1,0:T(8,128)(2,1)S(1)} %fusion.38), slice={[1:9:2], [1:17:2], [2:17:2], [0:256:1]} | slice | bytes 262144 | tf_op jit(solution)/shard_map/slice | solution.py:21
  63.4 9.7 %slice.143 = bf16[4,8,8,256]{3,2,1,0:T(8,128)(2,1)} slice(bf16[10,17,17,256]{3,2,1,0:T(8,128)(2,1)S(1)} %fusion.38), slice={[1:9:2], [1:17:2], [1:17:2], [0:256:1]} | slice | bytes 262144 | tf_op jit(solution)/shard_map/slice | solution.py:21
  73.1 9.7 %slice.142 = bf16[4,8,8,256]{3,2,1,0:T(8,128)(2,1)} slice(bf16[10,17,17,256]{3,2,1,0:T(8,128)(2,1)S(1)} %fusion.38), slice={[1:9:2], [1:17:2], [0:16:2], [0:256:1]} | slice | bytes 262144 | tf_op jit(solution)/shard_map/slice | solution.py:21
  82.8 9.7 %slice.141 = bf16[4,8,8,256]{3,2,1,0:T(8,128)(2,1)} slice(bf16[10,17,17,256]{3,2,1,0:T(8,128)(2,1)S(1)} %fusion.38), slice={[1:9:2], [0:16:2], [2:17:2], [0:256:1]} | slice | bytes 262144 | tf_op jit(solution)/shard_map/slice | solution.py:21
  92.5 9.7 %slice.140 = bf16[4,8,8,256]{3,2,1,0:T(8,128)(2,1)} slice(bf16[10,17,17,256]{3,2,1,0:T(8,128)(2,1)S(1)} %fusion.38), slice={[1:9:2], [0:16:2], [1:17:2], [0:256:1]} | slice | bytes 262144 | tf_op jit(solution)/shard_map/slice | solution.py:21
  102.2 9.7 %slice.139 = bf16[4,8,8,256]{3,2,1,0:T(8,128)(2,1)} slice(bf16[10,17,17,256]{3,2,1,0:T(8,128)(2,1)S(1)} %fusion.38), slice={[1:9:2], [0:16:2], [0:16:2], [0:256:1]} | slice | bytes 262144 | tf_op jit(solution)/shard_map/slice | solution.py:21
  111.9 9.8 %slice.138 = bf16[4,8,8,256]{3,2,1,0:T(8,128)(2,1)} slice(bf16[10,17,17,256]{3,2,1,0:T(8,128)(2,1)S(1)} %fusion.38), slice={[0:8:2], [2:17:2], [2:17:2], [0:256:1]} | slice | bytes 262144 | tf_op jit(solution)/shard_map/slice | solution.py:21
  121.7 9.7 %slice.137 = bf16[4,8,8,256]{3,2,1,0:T(8,128)(2,1)} slice(bf16[10,17,17,256]{3,2,1,0:T(8,128)(2,1)S(1)} %fusion.38), slice={[0:8:2], [2:17:2], [1:17:2], [0:256:1]} | slice | bytes 262144 | tf_op jit(solution)/shard_map/slice | solution.py:21
  131.4 9.7 %slice.136 = bf16[4,8,8,256]{3,2,1,0:T(8,128)(2,1)} slice(bf16[10,17,17,256]{3,2,1,0:T(8,128)(2,1)S(1)} %fusion.38), slice={[0:8:2], [2:17:2], [0:16:2], [0:256:1]} | slice | bytes 262144 | tf_op jit(solution)/shard_map/slice | solution.py:21
  141.1 9.8 %slice.135 = bf16[4,8,8,256]{3,2,1,0:T(8,128)(2,1)} slice(bf16[10,17,17,256]{3,2,1,0:T(8,128)(2,1)S(1)} %fusion.38), slice={[0:8:2], [1:17:2], [2:17:2], [0:256:1]} | slice | bytes 262144 | tf_op jit(solution)/shard_map/slice | solution.py:21
  150.9 9.7 %slice.134 = bf16[4,8,8,256]{3,2,1,0:T(8,128)(2,1)} slice(bf16[10,17,17,256]{3,2,1,0:T(8,128)(2,1)S(1)} %fusion.38), slice={[0:8:2], [1:17:2], [1:17:2], [0:256:1]} | slice | bytes 262144 | tf_op jit(solution)/shard_map/slice | solution.py:21
  160.6 9.7 %slice.133 = bf16[4,8,8,256]{3,2,1,0:T(8,128)(2,1)} slice(bf16[10,17,17,256]{3,2,1,0:T(8,128)(2,1)S(1)} %fusion.38), slice={[0:8:2], [1:17:2], [0:16:2], [0:256:1]} | slice | bytes 262144 | tf_op jit(solution)/shard_map/slice | solution.py:21
  170.3 9.8 %slice.132 = bf16[4,8,8,256]{3,2,1,0:T(8,128)(2,1)} slice(bf16[10,17,17,256]{3,2,1,0:T(8,128)(2,1)S(1)} %fusion.38), slice={[0:8:2], [0:16:2], [2:17:2], [0:256:1]} | slice | bytes 262144 | tf_op jit(solution)/shard_map/slice | solution.py:21
  180.1 9.7 %slice.131 = bf16[4,8,8,256]{3,2,1,0:T(8,128)(2,1)} slice(bf16[10,17,17,256]{3,2,1,0:T(8,128)(2,1)S(1)} %fusion.38), slice={[0:8:2], [0:16:2], [1:17:2], [0:256:1]} | slice | bytes 262144 | tf_op jit(solution)/shard_map/slice | solution.py:21
  189.8 9.7 %slice.130 = bf16[4,8,8,256]{3,2,1,0:T(8,128)(2,1)} slice(bf16[10,17,17,256]{3,2,1,0:T(8,128)(2,1)S(1)} %fusion.38), slice={[0:8:2], [0:16:2], [0:16:2], [0:256:1]} | slice | bytes 262144 | tf_op jit(solution)/shard_map/slice | solution.py:21
  212.5 1.7 copy-done.3
  214.3 4.1 %fusion.43 = f32[6912,256]{1,0:T(8,128)} fusion(bf16[256,6912]{1,0:T(8,128)(2,1)S(1)} %constant_dynamic-update-slice_fusion, bf16[256,256]{1,0:T(8,128)(2,1)S(1)} %bitcast.127), kind=kOutput, calls=%fused_computation.105 | convolution fusion | flops 905969664 | bytes 10747904 | tf_op jit(solution)/shard_map/dot_general | solution.py:119
  218.9 3.1 convolution_bitcast_fusion
  228.8 3.1 copy.39
  231.9 3.5 reshape.271
  238.2 1.9 slice_bitcast_fusion.7
  240.2 3.9 convolution_convert_fusion
  247.1 13.6 %all-reduce.10 = (f32[32]{0:T(128)S(1)}, f32[32]{0:T(128)S(1)}) all-reduce(f32[32]{0:T(128)S(1)} %reduce_sum.75, f32[32]{0:T(128)S(1)} %reduce_sum.72), channel_id=1, replica_groups=mesh['dp'=8,'tm'=4] {'tm'}, use_global_device_ids=true, to_apply=%region_11.12 | all-reduce | flops 64 | bytes 512 | tf_op jit(solution)/shard_map/psum | solution.py:107
  261.0 92.3 %reduce-scatter.2.cloned.1.call-done = f32[864,256]{1,0:T(8,128)} async-done(((f32[6912,256]{1,0:T(8,128)}), f32[864,256]{1,0:T(8,128)}) %reduce-scatter.2.cloned.1.call-update) | async-done | bytes 884752 | tf_op jit(solution)/shard_map/reduce_scatter | solution.py:123
  353.3 1.6 fusion.37
  354.9 35.1 %all-reduce.14.cloned.1.call-done = f32[864,256]{1,0:T(8,128)} async-done(((f32[864,256]{1,0:T(8,128)}), f32[864,256]{1,0:T(8,128)}) %all-reduce.14.cloned.1.call-update) | async-done | bytes 884752 | tf_op jit(solution)/shard_map/psum | solution.py:122
  390.0 2.1 copy.76
  (112 shorter events, 39.9 us)
Async XLA Ops:
  7.2 205.4 %copy-start = (bf16[1,4,8,8,256]{4,3,2,1,0:T(8,128)(2,1)S(1)}, bf16[1,4,8,8,256]{4,3,2,1,0:T(8,128)(2,1)}, u32[]{:S(2)}) copy-start(bf16[1,4,8,8,256]{4,3,2,1,0:T(8,128)(2,1)} %param.11) | copy-start | bytes 393220
  7.2 211.7 %all-gather.2.cloned.1.call-start = ((), (), s32[]{:S(2)}) async-start(), calls=%async_computation.1 | async-start | bytes 3981312 | tf_op jit(solution)/shard_map/all_gather | solution.py:95
  7.9 345.4 %reduce-scatter.2.cloned.1.call-start = ((), (), s32[]{:S(2)}) async-start(), calls=%async_computation.2 | async-start | bytes 7962624 | tf_op jit(solution)/shard_map/reduce_scatter | solution.py:123
  21.7 2.4 collective-permute-start
  201.1 11.1 %copy-start.9 = (bf16[4,8,8,256]{3,2,1,0:T(8,128)(2,1)S(1)}, bf16[4,8,8,256]{3,2,1,0:T(8,128)(2,1)}, u32[]{:S(2)}) copy-start(bf16[4,8,8,256]{3,2,1,0:T(8,128)(2,1)} %slice.142) | copy-start | bytes 393220
  201.1 11.2 %copy-start.8 = (bf16[4,8,8,256]{3,2,1,0:T(8,128)(2,1)S(1)}, bf16[4,8,8,256]{3,2,1,0:T(8,128)(2,1)}, u32[]{:S(2)}) copy-start(bf16[4,8,8,256]{3,2,1,0:T(8,128)(2,1)} %slice.143) | copy-start | bytes 393220
  201.1 11.2 %copy-start.7 = (bf16[4,8,8,256]{3,2,1,0:T(8,128)(2,1)S(1)}, bf16[4,8,8,256]{3,2,1,0:T(8,128)(2,1)}, u32[]{:S(2)}) copy-start(bf16[4,8,8,256]{3,2,1,0:T(8,128)(2,1)} %slice.144) | copy-start | bytes 393220
  201.1 11.2 %copy-start.6 = (bf16[4,8,8,256]{3,2,1,0:T(8,128)(2,1)S(1)}, bf16[4,8,8,256]{3,2,1,0:T(8,128)(2,1)}, u32[]{:S(2)}) copy-start(bf16[4,8,8,256]{3,2,1,0:T(8,128)(2,1)} %slice.145) | copy-start | bytes 393220
  201.1 11.2 %copy-start.5 = (bf16[4,8,8,256]{3,2,1,0:T(8,128)(2,1)S(1)}, bf16[4,8,8,256]{3,2,1,0:T(8,128)(2,1)}, u32[]{:S(2)}) copy-start(bf16[4,8,8,256]{3,2,1,0:T(8,128)(2,1)} %slice.146) | copy-start | bytes 393220
  212.5 1.8 copy-start.3
  218.4 171.6 %all-reduce.14.cloned.1.call-start = ((), (), s32[]{:S(2)}) async-start(), calls=%async_computation.3 | async-start | bytes 1769472 | tf_op jit(solution)/shard_map/psum | solution.py:122
  235.4 4.8 %copy-start.4 = (bf16[256,6912]{1,0:T(8,128)(2,1)S(1)}, bf16[256,6912]{1,0:T(8,128)(2,1)}, u32[]{:S(2)}) copy-start(bf16[256,6912]{1,0:T(8,128)(2,1)} %copy-done.3) | copy-start | bytes 10616836
  236.7 7.3 %collective-permute-start.1 = (f32[2,16,16,256]{3,2,1,0:T(8,128)S(1)}, f32[2,16,16,256]{3,2,1,0:T(8,128)S(1)}, u32[]{:S(2)}, u32[]{:S(2)}) collective-permute-start(f32[2,16,16,256]{3,2,1,0:T(8,128)S(1)} %slice.183), channel_id=1, source_target_pairs={{1,0},{2,1},{3,2},{5,4},{6,5},{7,6},{9,8},{10,9},{11,10},{13,12},{... | collective-permute-start | bytes 1572872 | tf_op jit(solution)/shard_map/ppermute | solution.py:13
  240.2 5.1 %copy-start.2 = (bf16[1,8,16,16,256]{4,3,2,1,0:T(8,128)(2,1)S(1)}, bf16[1,8,16,16,256]{4,3,2,1,0:T(8,128)(2,1)}, u32[]{:S(2)}) copy-start(bf16[1,8,16,16,256]{4,3,2,1,0:T(8,128)(2,1)} %param.6) | copy-start | bytes 3145732
  240.2 5.1 %copy-start.10 = (f32[256]{0:T(256)S(1)}, f32[256]{0:T(256)}, u32[]{:S(2)}) copy-start(f32[256]{0:T(256)} %param.10) | copy-start | bytes 3076
  240.2 5.1 %copy-start.11 = (f32[256]{0:T(256)S(1)}, f32[256]{0:T(256)}, u32[]{:S(2)}) copy-start(f32[256]{0:T(256)} %param.9) | copy-start | bytes 3076
  353.3 38.8 %copy-start.1 = (bf16[1,4,8,8,256]{4,3,2,1,0:T(8,128)(2,1)S(1)}, bf16[1,4,8,8,256]{4,3,2,1,0:T(8,128)(2,1)}, u32[]{:S(2)}) copy-start(bf16[1,4,8,8,256]{4,3,2,1,0:T(8,128)(2,1)} %param.11) | copy-start | bytes 393220
Sparse Core Ops, SparseCore 0:
  10.2 67.8 all-gather.1
  218.5 134.7 reduce-scatter.1
  355.8 34.1 all-reduce.13
where the time goes:
time: 399 us
  local copies, waits for them, and re-layouts  206 us (52%)
  waiting for transfers between devices  129 us (32%)
  blocking collectives  21.9 us (5%)
  between operations  15.1 us (4%)
  other arithmetic  12.5 us (3%)
  matrix products  11 us (3%)
    slice x27, local copies, waits for them, and re-layouts, unfold(): padded[step_t:step_t + 2 * frames_out:2, step_r:step_r + 2 * rows_out:2,...  176 us
    reduce_scatter x1, waiting for transfers between devices, shards(): lax.psum_scatter(clip_grad, 'dp', scatter_dimension=0, tiled=True)  92.3 us
    psum x1, waiting for transfers between devices, shards(): clip_grad = lax.psum(local_grad, 'tm')  35.1 us
    unnamed x51, local copies, waits for them, and re-layouts  15.1 us
    psum x1, blocking collectives, shards(): lax.psum((jnp.sum(grad_norm, axis=(0, 1, 2, 4)), jnp.sum(grad_norm * norm...  13.6 us
    psum x1, blocking collectives, shards(): lax.psum((jnp.sum(values * mask_group, axis=(0, 1, 2, 4)), jnp.sum(values...  8.37 us
  transfers between devices with their start and end apart: 5, of which 3 were waited for; matrix products, arithmetic and copies ran while one was open for 57% of the time, Pallas kernels for 0%

commit v1 on v0

--- a/solution.py
+++ b/solution.py
@@ -119,7 +119,7 @@
     local_grad = lax.dot_general(
         patches, cot_rows, (((0,), (0,)), ((), ())), preferred_element_type=jnp.float32
     )
-    clip_grad = lax.psum(local_grad, "tm")
+    clip_grad = jnp.sum(lax.all_gather(local_grad, "tm"), axis=0)
     weight_grad = lax.psum_scatter(clip_grad, "dp", scatter_dimension=0, tiled=True)
     return (out_block[None], input_grad[None], weight_grad)
 

time: 399 us -> 603 us (1.51)
  waiting for transfers between devices: 129 us -> 323 us
  other arithmetic: 12.5 us -> 27.5 us
    all_gather x0 -> x1, waiting for transfers between devices: none -> 177 us  [shards(): clip_grad = jnp.sum(lax.all_gather(local_grad, 'tm'), axis=0)]
    all_gather x1, waiting for transfers between devices: 0.02 us -> 52.1 us  [shards(): full_weight = lax.all_gather(weight, 'dp', axis=0, tiled=True)]
    psum x1 -> x0, waiting for transfers between devices: 35.1 us -> none  [shards(): clip_grad = lax.psum(local_grad, 'tm')]
    reduce_sum x0 -> x1, other arithmetic: none -> 15 us  [shards(): clip_grad = jnp.sum(lax.all_gather(local_grad, 'tm'), axis=0)]
    unnamed x51 -> x46, local copies, waits for them, and re-layouts: 15.1 us -> 14.8 us
  transfers between devices with their start and end apart: 5 -> 5, of which waited for: 3 -> 4; matrix products, arithmetic and copies ran while one was open for 57% -> 7% of each run, Pallas kernels for 0% -> 0%
where the time goes in v1:
time: 603 us
  waiting for transfers between devices  323 us (54%)
  local copies, waits for them, and re-layouts  205 us (34%)
  other arithmetic  27.5 us (5%)
  blocking collectives  17.8 us (3%)
  between operations  15 us (2%)
  matrix products  11 us (2%)
    all_gather x1, waiting for transfers between devices, shards(): clip_grad = jnp.sum(lax.all_gather(local_grad, 'tm'), axis=0)  177 us
    slice x27, local copies, waits for them, and re-layouts, unfold(): padded[step_t:step_t + 2 * frames_out:2, step_r:step_r + 2 * rows_out:2,...  176 us
    reduce_scatter x1, waiting for transfers between devices, shards(): lax.psum_scatter(clip_grad, 'dp', scatter_dimension=0, tiled=True)  92.2 us
    all_gather x1, waiting for transfers between devices, shards(): full_weight = lax.all_gather(weight, 'dp', axis=0, tiled=True)  52.1 us
    reduce_sum x1, other arithmetic, shards(): clip_grad = jnp.sum(lax.all_gather(local_grad, 'tm'), axis=0)  15 us
    unnamed x46, local copies, waits for them, and re-layouts  14.8 us
  transfers between devices with their start and end apart: 5, of which 4 were waited for; matrix products, arithmetic and copies ran while one was open for 7% of the time, Pallas kernels for 0%

profile of v1, /device:TPU:0, one launch (start us, length us, event | category | flops | bytes accessed | tf_op | source)
XLA Modules:
  0.0 602.8 jit_solution(7198181999939417145)
XLA Ops:
  7.9 1.8 fusion.18
  10.2 8.4 %all-reduce.11 = (f32[32]{0:T(128)S(1)}, f32[32]{0:T(128)S(1)}) all-reduce(f32[32]{0:T(128)S(1)} %reduce_sum.59, f32[32]{0:T(128)S(1)} %reduce_sum.62), channel_id=1, replica_groups=mesh['dp'=8,'tm'=4] {'tm'}, use_global_device_ids=true, to_apply=%region_2.0 | all-reduce | flops 64 | bytes 512 | tf_op jit(solution)/shard_map/psum | solution.py:76
  18.9 2.0 fusion.15
  24.4 9.8 %slice.130 = bf16[4,8,8,256]{3,2,1,0:T(8,128)(2,1)} slice(bf16[10,17,17,256]{3,2,1,0:T(8,128)(2,1)S(1)} %fusion.38), slice={[0:8:2], [0:16:2], [0:16:2], [0:256:1]} | slice | bytes 262144 | tf_op jit(solution)/shard_map/slice | solution.py:21
  34.2 9.7 %slice.131 = bf16[4,8,8,256]{3,2,1,0:T(8,128)(2,1)} slice(bf16[10,17,17,256]{3,2,1,0:T(8,128)(2,1)S(1)} %fusion.38), slice={[0:8:2], [0:16:2], [1:17:2], [0:256:1]} | slice | bytes 262144 | tf_op jit(solution)/shard_map/slice | solution.py:21
  44.0 9.8 %slice.132 = bf16[4,8,8,256]{3,2,1,0:T(8,128)(2,1)} slice(bf16[10,17,17,256]{3,2,1,0:T(8,128)(2,1)S(1)} %fusion.38), slice={[0:8:2], [0:16:2], [2:17:2], [0:256:1]} | slice | bytes 262144 | tf_op jit(solution)/shard_map/slice | solution.py:21
  53.7 9.7 %slice.133 = bf16[4,8,8,256]{3,2,1,0:T(8,128)(2,1)} slice(bf16[10,17,17,256]{3,2,1,0:T(8,128)(2,1)S(1)} %fusion.38), slice={[0:8:2], [1:17:2], [0:16:2], [0:256:1]} | slice | bytes 262144 | tf_op jit(solution)/shard_map/slice | solution.py:21
  63.5 9.7 %slice.134 = bf16[4,8,8,256]{3,2,1,0:T(8,128)(2,1)} slice(bf16[10,17,17,256]{3,2,1,0:T(8,128)(2,1)S(1)} %fusion.38), slice={[0:8:2], [1:17:2], [1:17:2], [0:256:1]} | slice | bytes 262144 | tf_op jit(solution)/shard_map/slice | solution.py:21
  73.2 9.8 %slice.135 = bf16[4,8,8,256]{3,2,1,0:T(8,128)(2,1)} slice(bf16[10,17,17,256]{3,2,1,0:T(8,128)(2,1)S(1)} %fusion.38), slice={[0:8:2], [1:17:2], [2:17:2], [0:256:1]} | slice | bytes 262144 | tf_op jit(solution)/shard_map/slice | solution.py:21
  82.9 9.7 %slice.136 = bf16[4,8,8,256]{3,2,1,0:T(8,128)(2,1)} slice(bf16[10,17,17,256]{3,2,1,0:T(8,128)(2,1)S(1)} %fusion.38), slice={[0:8:2], [2:17:2], [0:16:2], [0:256:1]} | slice | bytes 262144 | tf_op jit(solution)/shard_map/slice | solution.py:21
  92.6 9.7 %slice.137 = bf16[4,8,8,256]{3,2,1,0:T(8,128)(2,1)} slice(bf16[10,17,17,256]{3,2,1,0:T(8,128)(2,1)S(1)} %fusion.38), slice={[0:8:2], [2:17:2], [1:17:2], [0:256:1]} | slice | bytes 262144 | tf_op jit(solution)/shard_map/slice | solution.py:21
  102.4 9.7 %slice.138 = bf16[4,8,8,256]{3,2,1,0:T(8,128)(2,1)} slice(bf16[10,17,17,256]{3,2,1,0:T(8,128)(2,1)S(1)} %fusion.38), slice={[0:8:2], [2:17:2], [2:17:2], [0:256:1]} | slice | bytes 262144 | tf_op jit(solution)/shard_map/slice | solution.py:21
  112.1 9.7 %slice.139 = bf16[4,8,8,256]{3,2,1,0:T(8,128)(2,1)} slice(bf16[10,17,17,256]{3,2,1,0:T(8,128)(2,1)S(1)} %fusion.38), slice={[1:9:2], [0:16:2], [0:16:2], [0:256:1]} | slice | bytes 262144 | tf_op jit(solution)/shard_map/slice | solution.py:21
  121.8 9.7 %slice.140 = bf16[4,8,8,256]{3,2,1,0:T(8,128)(2,1)} slice(bf16[10,17,17,256]{3,2,1,0:T(8,128)(2,1)S(1)} %fusion.38), slice={[1:9:2], [0:16:2], [1:17:2], [0:256:1]} | slice | bytes 262144 | tf_op jit(solution)/shard_map/slice | solution.py:21
  131.5 9.7 %slice.141 = bf16[4,8,8,256]{3,2,1,0:T(8,128)(2,1)} slice(bf16[10,17,17,256]{3,2,1,0:T(8,128)(2,1)S(1)} %fusion.38), slice={[1:9:2], [0:16:2], [2:17:2], [0:256:1]} | slice | bytes 262144 | tf_op jit(solution)/shard_map/slice | solution.py:21
  141.3 9.7 %slice.142 = bf16[4,8,8,256]{3,2,1,0:T(8,128)(2,1)} slice(bf16[10,17,17,256]{3,2,1,0:T(8,128)(2,1)S(1)} %fusion.38), slice={[1:9:2], [1:17:2], [0:16:2], [0:256:1]} | slice | bytes 262144 | tf_op jit(solution)/shard_map/slice | solution.py:21
  151.0 9.7 %slice.143 = bf16[4,8,8,256]{3,2,1,0:T(8,128)(2,1)} slice(bf16[10,17,17,256]{3,2,1,0:T(8,128)(2,1)S(1)} %fusion.38), slice={[1:9:2], [1:17:2], [1:17:2], [0:256:1]} | slice | bytes 262144 | tf_op jit(solution)/shard_map/slice | solution.py:21
  160.7 9.8 %slice.144 = bf16[4,8,8,256]{3,2,1,0:T(8,128)(2,1)} slice(bf16[10,17,17,256]{3,2,1,0:T(8,128)(2,1)S(1)} %fusion.38), slice={[1:9:2], [1:17:2], [2:17:2], [0:256:1]} | slice | bytes 262144 | tf_op jit(solution)/shard_map/slice | solution.py:21
  170.5 9.7 %slice.145 = bf16[4,8,8,256]{3,2,1,0:T(8,128)(2,1)} slice(bf16[10,17,17,256]{3,2,1,0:T(8,128)(2,1)S(1)} %fusion.38), slice={[1:9:2], [2:17:2], [0:16:2], [0:256:1]} | slice | bytes 262144 | tf_op jit(solution)/shard_map/slice | solution.py:21
  180.2 9.7 %slice.146 = bf16[4,8,8,256]{3,2,1,0:T(8,128)(2,1)} slice(bf16[10,17,17,256]{3,2,1,0:T(8,128)(2,1)S(1)} %fusion.38), slice={[1:9:2], [2:17:2], [1:17:2], [0:256:1]} | slice | bytes 262144 | tf_op jit(solution)/shard_map/slice | solution.py:21
  213.5 1.8 copy-done.3
  215.3 4.0 fusion.43
  220.3 176.8 %all-gather.6.cloned.1.call-done = f32[27648,256]{1,0:T(8,128)} async-done(((f32[6912,256]{1,0:T(8,128)}), f32[27648,256]{1,0:T(8,128)}) %all-gather.6.cloned.1.call-update) | async-done | bytes 28311568 | tf_op jit(solution)/shard_map/all_gather | solution.py:122
  397.1 15.0 %reduce_sum.85 = f32[6912,256]{1,0:T(8,128)} reduce(f32[4,6912,256]{2,1,0:T(8,128)} %bitcast.129, f32[]{:T(128)} %constant.4.clone.1), dimensions={0}, to_apply=%region_12.13 | reduce | flops 5308416 | bytes 35389444 | tf_op jit(solution)/shard_map/reduce_sum | solution.py:122
  412.4 52.1 %all-gather.4.cloned.1.call-done = bf16[6912,256]{1,0:T(8,128)(2,1)} async-done(((bf16[864,256]{1,0:T(8,128)(2,1)}), bf16[6912,256]{1,0:T(8,128)(2,1)}) %all-gather.4.cloned.1.call-update) | async-done | bytes 3538960 | tf_op jit(solution)/shard_map/all_gather | solution.py:95
  464.5 3.1 convolution_bitcast_fusion
  474.3 3.1 copy.39
  477.4 3.5 reshape.271
  483.8 1.9 slice_bitcast_fusion.7
  485.8 3.9 convolution_convert_fusion
  492.7 9.5 %all-reduce.10 = (f32[32]{0:T(128)S(1)}, f32[32]{0:T(128)S(1)}) all-reduce(f32[32]{0:T(128)S(1)} %reduce_sum.84, f32[32]{0:T(128)S(1)} %reduce_sum.81), channel_id=1, replica_groups=mesh['dp'=8,'tm'=4] {'tm'}, use_global_device_ids=true, to_apply=%region_11.12 | all-reduce | flops 64 | bytes 512 | tf_op jit(solution)/shard_map/psum | solution.py:107
  504.1 92.2 %reduce-scatter.2.cloned.1.call-done = f32[864,256]{1,0:T(8,128)} async-done(((f32[6912,256]{1,0:T(8,128)}), f32[864,256]{1,0:T(8,128)}) %reduce-scatter.2.cloned.1.call-update) | async-done | bytes 884752 | tf_op jit(solution)/shard_map/reduce_scatter | solution.py:123
  (108 shorter events, 43.3 us)
Async XLA Ops:
  7.2 206.3 %copy-start = (bf16[1,4,8,8,256]{4,3,2,1,0:T(8,128)(2,1)S(1)}, bf16[1,4,8,8,256]{4,3,2,1,0:T(8,128)(2,1)}, u32[]{:S(2)}) copy-start(bf16[1,4,8,8,256]{4,3,2,1,0:T(8,128)(2,1)} %param.11) | copy-start | bytes 393220
  7.2 389.9 %all-gather.6.cloned.1.call-start = ((), (), s32[]{:S(2)}) async-start(), calls=%async_computation.3 | async-start | bytes 35389440 | tf_op jit(solution)/shard_map/all_gather | solution.py:122
  21.0 2.4 collective-permute-start
  200.3 12.9 %copy-start.7 = (bf16[4,8,8,256]{3,2,1,0:T(8,128)(2,1)S(1)}, bf16[4,8,8,256]{3,2,1,0:T(8,128)(2,1)}, u32[]{:S(2)}) copy-start(bf16[4,8,8,256]{3,2,1,0:T(8,128)(2,1)} %slice.144) | copy-start | bytes 393220
  200.3 13.0 %copy-start.6 = (bf16[4,8,8,256]{3,2,1,0:T(8,128)(2,1)S(1)}, bf16[4,8,8,256]{3,2,1,0:T(8,128)(2,1)}, u32[]{:S(2)}) copy-start(bf16[4,8,8,256]{3,2,1,0:T(8,128)(2,1)} %slice.145) | copy-start | bytes 393220
  200.3 13.0 %copy-start.5 = (bf16[4,8,8,256]{3,2,1,0:T(8,128)(2,1)S(1)}, bf16[4,8,8,256]{3,2,1,0:T(8,128)(2,1)}, u32[]{:S(2)}) copy-start(bf16[4,8,8,256]{3,2,1,0:T(8,128)(2,1)} %slice.146) | copy-start | bytes 393220
  213.5 1.8 copy-start.3
  219.3 245.2 %all-gather.4.cloned.1.call-start = ((), (), s32[]{:S(2)}) async-start(), calls=%async_computation.1 | async-start | bytes 3981312 | tf_op jit(solution)/shard_map/all_gather | solution.py:95
  220.0 376.2 %reduce-scatter.2.cloned.1.call-start = ((), (), s32[]{:S(2)}) async-start(), calls=%async_computation.2 | async-start | bytes 7962624 | tf_op jit(solution)/shard_map/reduce_scatter | solution.py:123
  480.9 4.8 copy-start.4
  482.3 7.3 %collective-permute-start.1 = (f32[2,16,16,256]{3,2,1,0:T(8,128)S(1)}, f32[2,16,16,256]{3,2,1,0:T(8,128)S(1)}, u32[]{:S(2)}, u32[]{:S(2)}) collective-permute-start(f32[2,16,16,256]{3,2,1,0:T(8,128)S(1)} %slice.183), channel_id=1, source_target_pairs={{1,0},{2,1},{3,2},{5,4},{6,5},{7,6},{9,8},{10,9},{11,10},{13,12},{... | collective-permute-start | bytes 1572872 | tf_op jit(solution)/shard_map/ppermute | solution.py:13
  485.7 5.2 copy-start.2
  485.7 5.2 copy-start.8
  485.8 5.2 copy-start.9
  489.6 106.6 %copy-start.1 = (bf16[1,4,8,8,256]{4,3,2,1,0:T(8,128)(2,1)S(1)}, bf16[1,4,8,8,256]{4,3,2,1,0:T(8,128)(2,1)}, u32[]{:S(2)}) copy-start(bf16[1,4,8,8,256]{4,3,2,1,0:T(8,128)(2,1)} %param.11) | copy-start | bytes 393220
Sparse Core Ops, SparseCore 0:
  219.4 177.6 all-gather.5
  399.3 65.1 all-gather.3
  468.8 127.4 reduce-scatter.1
